TPU v7x, 128 devices: a whole 4x4x4 slice. The times are simulated.
128 devices in a mesh: role: 2 (over core), dev: 64 (over z, y, x).
Axes of the slice: x: 4, y: 4, z: 4, core: 2. Of those that a mesh axis runs over, the one named last changes fastest.
Arguments:
- moe_rows: bfloat16 [4096, 3584], P(('role', 'dev')), may hold values from -6 to 6
- expert_ids: int32 [4096, 8], P(('role', 'dev')), may hold values from 0 to 63, all different within a row; in each aligned block of 32 rows (0 to 31, 32 to 63, ...) at most 8 rows name the same one
- gate_weights: float32 [4096, 8], P(('role', 'dev')), may hold values from 0.05 to 0.6
- w_gate: bfloat16 [64, 3584, 1024], P('dev', None, 'role'), may hold values from -0.09375 to 0.09375
- w_up: bfloat16 [64, 3584, 1024], P('dev', None, 'role'), may hold values from -0.09375 to 0.09375
- w_down: bfloat16 [64, 3584, 1024], P('dev', None, 'role'), may hold values from -0.1875 to 0.1875
- q_latent: bfloat16 [512, 64, 512], P(('role', 'dev')), may hold values from -40 to 40
- q_rope: bfloat16 [512, 4096], P(('role', 'dev')), may hold values from -4 to 4
- latent_cache: bfloat16 [512, 2048, 512], P(('role', 'dev')), may hold values from -4 to 4
- rope_cache: bfloat16 [512, 64, 2048], P(('role', 'dev')), may hold values from -4 to 4
- lengths: int32 [512], P(('role', 'dev')), may hold values from 2 to 2048, as said below
Outputs:
- moe_out: bfloat16 [4096, 3584], P(('role', 'dev'))
- attended: bfloat16 [512, 64, 512], P(('role', 'dev'))
Inputs may be any that keep to these rules, and one draw needn't show every extreme that they name: `expert_ids`: each row names 8 different experts; among the rows of one device no expert is named more than 8 times. `lengths`: the first row holds all 2048 cached tokens.
All inputs are finite; a program needn't handle non-finite values.
Results may differ from a plain program's by a relative error of at most 0.0057.
Values may be sent and summed in bfloat16 or wider, within the bound.
A program may use at most 128 MiB of HBM per device.

v0:
```python
import jax
import jax.numpy as jnp
from jax import lax
from jax.sharding import PartitionSpec as P

score_scale = 192.0 ** (-0.5)


def expert_block(chosen, gate_matrix, up_matrix, down_matrix):
    gate_part = jnp.dot(chosen, gate_matrix, preferred_element_type=jnp.float32)
    up_part = jnp.dot(chosen, up_matrix, preferred_element_type=jnp.float32)
    hidden_units = (jax.nn.silu(gate_part) * up_part).astype(jnp.bfloat16)
    return lax.dot_general(
        hidden_units, down_matrix, (((1,), (1,)), ((), ())), preferred_element_type=jnp.float32
    )


def attend_row(query_lat, query_rope, cache_lat, cache_rope, length):
    head_count = query_lat.shape[0]
    rope_width = cache_rope.shape[0]
    scores = lax.dot_general(
        query_lat, cache_lat, (((1,), (1,)), ((), ())), preferred_element_type=jnp.float32
    )
    scores = scores + jnp.dot(
        query_rope.reshape(head_count, rope_width), cache_rope, preferred_element_type=jnp.float32
    )
    scores = scores * score_scale
    positions = jnp.arange(cache_lat.shape[0], dtype=jnp.int32)
    valid = (positions < length)[None, :]
    scores = jnp.where(valid, scores, jnp.float32(-1e30))
    highest = jnp.max(scores, axis=1, keepdims=True)
    weights = jnp.where(valid, jnp.exp(scores - highest), jnp.float32(0.0))
    probs = (weights / jnp.sum(weights, axis=1, keepdims=True)).astype(jnp.bfloat16)
    return jnp.dot(probs, cache_lat, preferred_element_type=jnp.float32).astype(jnp.bfloat16)


def per_device(
    moe_rows,
    expert_ids,
    gate_weights,
    w_gate,
    w_up,
    w_down,
    q_latent,
    q_rope,
    latent_cache,
    rope_cache,
    lengths,
):
    tok_count = moe_rows.shape[0]
    width = moe_rows.shape[1]
    topk_count = expert_ids.shape[1]
    experts = lax.axis_size("dev")
    capacity = min(tok_count, 2 * tok_count * topk_count // experts)
    flat_ids = expert_ids.reshape(-1)
    pair_count = flat_ids.shape[0]
    one_hot = (flat_ids[:, None] == jnp.arange(experts, dtype=jnp.int32)[None, :]).astype(jnp.int32)
    earlier = jnp.cumsum(one_hot, axis=0) - one_hot
    slot_index = jnp.sum(earlier * one_hot, axis=1)
    destination = flat_ids * capacity + slot_index
    source_row = jnp.full((experts * capacity,), tok_count, jnp.int32)
    source_row = source_row.at[destination].set(
        jnp.arange(pair_count, dtype=jnp.int32) // topk_count
    )
    padded_rows = jnp.concatenate([moe_rows, jnp.zeros((1, width), jnp.bfloat16)], axis=0)
    outgoing = padded_rows[source_row].reshape(experts, capacity, width)
    arrived = lax.all_to_all(outgoing, "dev", split_axis=0, concat_axis=0, tiled=True)
    own_rows = arrived.reshape(experts * capacity, width)
    both_rows = lax.all_gather(own_rows, "role", axis=0, tiled=True)
    expert_sum = lax.psum_scatter(
        expert_block(both_rows, w_gate[0], w_up[0], w_down[0]),
        "role",
        scatter_dimension=0,
        tiled=True,
    )
    finished = expert_sum.astype(jnp.bfloat16).reshape(experts, capacity, width)
    returned = lax.all_to_all(finished, "dev", split_axis=0, concat_axis=0, tiled=True)
    flat_back = returned.reshape(experts * capacity, width)
    picked = flat_back[destination].reshape(tok_count, topk_count, width).astype(jnp.float32)
    moe_out = jnp.sum(picked * gate_weights[:, :, None], axis=1).astype(jnp.bfloat16)
    attended = jax.vmap(attend_row)(q_latent, q_rope, latent_cache, rope_cache, lengths)
    return (moe_out, attended)


def solution(mesh):
    placed = (
        P(("role", "dev"), None),
        P(("role", "dev"), None),
        P(("role", "dev"), None),
        P("dev", None, "role"),
        P("dev", None, "role"),
        P("dev", None, "role"),
        P(("role", "dev"), None, None),
        P(("role", "dev"), None),
        P(("role", "dev"), None, None),
        P(("role", "dev"), None, None),
        P(("role", "dev")),
    )
    return jax.shard_map(
        per_device,
        mesh=mesh,
        in_specs=placed,
        out_specs=(P(("role", "dev"), None), P(("role", "dev"), None, None)),
        check_vma=False,
    )
```

profile of v0, /device:TPU:1, one launch (start us, length us, event | category | flops | bytes accessed | tf_op | source)
XLA Modules:
  0.0 223.4 jit_solution(7646429509567561305)
XLA Ops:
  7.2 0.0 copy-start
  7.2 0.0 all-gather.2.cloned.1.call-start
  7.2 0.8 copy.15
  8.1 0.1 eq.29
  8.2 0.1 eq.25
  8.2 0.7 broadcast_multiply_fusion
  9.0 0.6 reduce-window.6
  9.6 0.2 slice_reduce_fusion
  9.8 0.1 copy.14
  9.9 0.1 mul.42
  10.0 0.1 fusion.21
  10.1 1.4 scatter_custom_fusion
  11.5 1.0 concatenate.3
  12.5 4.2 %gather_fusion = bf16[512,3584]{1,0:T(8,128)(2,1)} fusion(bf16[33,3584]{1,0:T(8,128)(2,1)S(1)} %concatenate.3, s32[1024]{0:T(1024)S(1)} %pad_clamp_fusion.1), kind=kCustom, calls=%fused_computation | custom fusion | bytes 7342080 | tf_op jit(solution)/shard_map/gather | solution.py:66
  16.7 57.5 %all_to_all.10 = bf16[64,8,3584]{2,1,0:T(8,128)(2,1)} all-to-all(bf16[64,8,3584]{2,1,0:T(8,128)(2,1)} %bitcast.49), channel_id=1, replica_groups=mesh['role'=2,'dev'=64] {'dev'}, dimensions={0} | all-to-all | bytes 7340032 | tf_op jit(solution)/shard_map/all_to_all | solution.py:67
  74.2 0.0 all-gather.2.cloned.1.call-update
  74.2 0.0 reduce-scatter.2.cloned.1.call-start
  74.3 19.5 %all-gather.2.cloned.1.call-done = bf16[1024,3584]{1,0:T(8,128)(2,1)} async-done(((bf16[512,3584]{1,0:T(8,128)(2,1)}), bf16[1024,3584]{1,0:T(8,128)(2,1)}) %all-gather.2.cloned.1.call-update) | async-done | bytes 7340048 | tf_op jit(solution)/shard_map/all_gather | solution.py:69
  93.8 7.3 %fusion.4 = f32[1024,512]{1,0:T(8,128)S(1)} fusion(bf16[1024,3584]{1,0:T(8,128)(2,1)} %all-gather.2.cloned.1.call-done, bf16[1,3584,512]{2,1,0:T(8,128)(2,1)} %param.15), kind=kOutput, calls=%fused_computation.8 | convolution fusion | flops 3758096384 | bytes 13107200 | tf_op jit(solution)/shard_map/dot_general | solution.py:11
  101.1 15.5 %fusion.2 = f32[1024,3584]{1,0:T(8,128)} fusion(bf16[1,3584,512]{2,1,0:T(8,128)(2,1)} %param.16, f32[1024,512]{1,0:T(8,128)S(1)} %fusion.4, bf16[1024,3584]{1,0:T(8,128)(2,1)} %all-gather.2.cloned.1.call-done, bf16[1,3584,512]{2,1,0:T(8,128)(2,1)} %param.14), kind=kOutput, calls=%fused_computation.6 | convolution fusion | flops 7519338496 | bytes 31457280 | tf_op jit(solution)/shard_map/dot_general | solution.py:13
  116.6 0.0 reduce-scatter.2.cloned.1.call-update
  116.6 28.2 %reduce-scatter.2.cloned.1.call-done = f32[512,3584]{1,0:T(8,128)} async-done(((f32[1024,3584]{1,0:T(8,128)}), f32[512,3584]{1,0:T(8,128)}) %reduce-scatter.2.cloned.1.call-update) | async-done | bytes 7340048 | tf_op jit(solution)/shard_map/reduce_scatter | solution.py:70
  144.8 5.3 %convert_bitcast_fusion = bf16[64,8,3584]{2,1,0:T(8,128)(2,1)} fusion(f32[512,3584]{1,0:T(8,128)} %reduce-scatter.2.cloned.1.call-done), kind=kLoop, calls=%fused_computation.12 | loop fusion | flops 1835008 | bytes 11010048 | tf_op jit(solution)/shard_map/reshape | solution.py:76
  150.1 0.0 copy-start.3
  150.1 0.0 copy-start.2
  150.1 0.0 copy-start.4
  150.1 0.0 copy-start.1
  150.1 10.7 %all-to-all-start.1 = ((bf16[64,8,3584]{2,1,0:T(8,128)(2,1)}), bf16[64,8,3584]{2,1,0:T(8,128)(2,1)}, u32[]{:S(2)}, u32[]{:S(2)}) async-start(bf16[64,8,3584]{2,1,0:T(8,128)(2,1)} %convert_bitcast_fusion), calls=%async_computation.2 | async-start | bytes 7340032 | tf_op jit(solution)/shard_map/all_to_all | solution.py:77
  160.8 0.0 copy-done.3
  160.8 0.1 copy.18
  160.8 0.0 copy-done.2
  160.8 0.1 reshape.93
  161.0 0.0 copy-done.4
  161.0 0.1 iota_compare_fusion.2
  161.1 0.0 copy-done.1
  161.1 6.0 %fusion.27 = f32[4,64,2048]{2,1,0:T(8,128)S(1)} fusion(bf16[4,64,512]{2,1,0:T(8,128)(2,1)S(1)} %copy-done.1, bf16[4,2048,512]{2,1,0:T(8,128)(2,1)} %param.19), kind=kOutput, calls=%fused_computation.47 | convolution fusion | flops 536870912 | bytes 10747904 | tf_op jit(solution)/shard_map/vmap()/dot_general | solution.py:21
  167.1 0.0 copy-done
  167.1 2.4 %fusion.26 = (f32[4,64]{1,0:T(4,128)S(1)}, f32[4,64,2048]{2,1,0:T(8,128)}) fusion(pred[4,2048]{1,0:T(4,128)(4,1)S(1)} %iota_compare_fusion.2, f32[4,64,2048]{2,1,0:T(8,128)S(1)} %fusion.27, bf16[4,64,64]{2,1,0:T(8,128)(2,1)S(1)} %reshape.93, bf16[4,64,2048]{2,1,0:T(8,128)(2,1)S(1)} %copy-done), kind=kOutput, calls=%fused_computation.46 | convolution fusion | flops 70256640 | bytes 5284864 | tf_op jit(solution)/shard_map/vmap()/sub | solution.py:32
  169.4 6.3 %convolution_convert_fusion = bf16[4,64,512]{2,1,0:T(8,128)(2,1)} fusion(bf16[4,2048,512]{2,1,0:T(8,128)(2,1)} %param.19, f32[4,64,2048]{2,1,0:T(8,128)} %get-tuple-element.3, f32[4,64]{1,0:T(4,128)S(1)} %get-tuple-element.2), kind=kOutput, calls=%fused_computation.21 | convolution fusion | flops 538050560 | bytes 10748928 | tf_op jit(solution)/shard_map/vmap()/dot_general | solution.py:34
  175.8 32.6 %all-to-all-done.1 = bf16[64,8,3584]{2,1,0:T(8,128)(2,1)} async-done(((bf16[64,8,3584]{2,1,0:T(8,128)(2,1)}), bf16[64,8,3584]{2,1,0:T(8,128)(2,1)}, u32[]{:S(2)}, u32[]{:S(2)}) %all-to-all-start.1) | async-done | bytes 3670048 | tf_op jit(solution)/shard_map/all_to_all | solution.py:77
  208.4 6.0 %gather_fusion.1 = bf16[256,3584]{1,0:T(8,128)(2,1)S(1)} fusion(bf16[512,3584]{1,0:T(8,128)(2,1)} %bitcast.9, s32[1024]{0:T(1024)S(1)} %pad_clamp_fusion), kind=kCustom, calls=%fused_computation.1 | custom fusion | bytes 3671040 | tf_op jit(solution)/shard_map/gather | solution.py:79
  214.5 2.1 fusion.1
  (8 shorter events, 0.1 us)
Async XLA Ops:
  7.2 159.9 %copy-start = (bf16[4,64,2048]{2,1,0:T(8,128)(2,1)S(1)}, bf16[4,64,2048]{2,1,0:T(8,128)(2,1)}, u32[]{:S(2)}) copy-start(bf16[4,64,2048]{2,1,0:T(8,128)(2,1)} %param.20) | copy-start | bytes 3145732
  7.2 86.6 %all-gather.2.cloned.1.call-start = ((), (), s32[]{:S(2)}) async-start(), calls=%async_computation.3 | async-start | bytes 11010048 | tf_op jit(solution)/shard_map/all_gather | solution.py:69
  74.2 70.5 %reduce-scatter.2.cloned.1.call-start = ((), (), s32[]{:S(2)}) async-start(), calls=%async_computation.4 | async-start | bytes 22020096 | tf_op jit(solution)/shard_map/reduce_scatter | solution.py:70
  150.1 10.7 %copy-start.3 = (f32[32,8]{0,1:T(8,128)S(1)}, f32[32,8]{0,1:T(8,128)}, u32[]{:S(2)}) copy-start(f32[32,8]{0,1:T(8,128)} %param.13) | copy-start | bytes 3076
  150.1 10.8 %copy-start.2 = (bf16[4,4096]{1,0:T(4,128)(2,1)S(1)}, bf16[4,4096]{1,0:T(4,128)(2,1)}, u32[]{:S(2)}) copy-start(bf16[4,4096]{1,0:T(4,128)(2,1)} %param.18) | copy-start | bytes 98308
  150.1 10.9 %copy-start.4 = (s32[4]{0:T(128)S(1)}, s32[4]{0:T(128)}, u32[]{:S(2)}) copy-start(s32[4]{0:T(128)} %param.21) | copy-start | bytes 52
  150.1 11.0 %copy-start.1 = (bf16[4,64,512]{2,1,0:T(8,128)(2,1)S(1)}, bf16[4,64,512]{2,1,0:T(8,128)(2,1)}, u32[]{:S(2)}) copy-start(bf16[4,64,512]{2,1,0:T(8,128)(2,1)} %param.17) | copy-start | bytes 786436
  150.1 58.3 %all-to-all-start.1 = ((bf16[64,8,3584]{2,1,0:T(8,128)(2,1)}), bf16[64,8,3584]{2,1,0:T(8,128)(2,1)}, u32[]{:S(2)}, u32[]{:S(2)}) async-start(bf16[64,8,3584]{2,1,0:T(8,128)(2,1)} %convert_bitcast_fusion), calls=%async_computation.2 | async-start | bytes 7340032 | tf_op jit(solution)/shard_map/all_to_all | solution.py:77
Sparse Core Ops, SparseCore 0:
  74.4 19.3 all-gather.1
  116.7 28.0 reduce-scatter.1
where the time goes:
time: 224 us; the launch traced here: 223 us
  waiting for transfers between devices  80.4 us (36%)
  blocking collectives  57.5 us (26%)
  matrix products  37.5 us (17%)
  local copies, waits for them, and re-layouts  14.2 us (6%)
  between operations  14.2 us (6%)
  starting transfers between devices  10.8 us (5%)
  other arithmetic  8.97 us (4%)
    all_to_all x1, blocking collectives, per_device(): lax.all_to_all(outgoing, 'dev', split_axis=0, concat_axis=0, tiled=True)  57.5 us
    all_to_all x1, waiting for transfers between devices, per_device(): lax.all_to_all(finished, 'dev', split_axis=0, concat_axis=0, tiled=True)  32.6 us
    reduce_scatter x1, waiting for transfers between devices, per_device(): lax.psum_scatter(expert_block(both_rows, w_gate[0], w_up[0], w_down[0]),...  28.2 us
    all_gather x1, waiting for transfers between devices, per_device(): both_rows = lax.all_gather(own_rows, 'role', axis=0, tiled=True)  19.5 us
    dot_general x1, matrix products, expert_block(): lax.dot_general(hidden_units, down_matrix, (((1,), (1,)), ((), ())), pref...  15.5 us
    all_to_all x1, starting transfers between devices, per_device(): lax.all_to_all(finished, 'dev', split_axis=0, concat_axis=0, tiled=True)  10.7 us
    dot_general x1, matrix products, expert_block(): up_part = jnp.dot(chosen, up_matrix, preferred_element_type=jnp.float32)  7.29 us
    dot_general x1, matrix products, attend_row(): jnp.dot(probs, cache_lat, preferred_element_type=jnp.float32)  6.34 us
  transfers between devices with their start and end apart: 3, of which 3 were waited for; matrix products, arithmetic and copies ran while one was open for 7% of the time, Pallas kernels for 0%

commit v1 on v0

--- a/solution.py
+++ b/solution.py
@@ -4,6 +4,14 @@
 from jax.sharding import PartitionSpec as P
 
 score_scale = 192.0 ** (-0.5)
+
+
+def gather_by_exchange(value, axis, dim):
+    size = lax.axis_size(axis)
+    repeats = [size if d == dim else 1 for d in range(value.ndim)]
+    return lax.all_to_all(
+        jnp.tile(value, repeats), axis, split_axis=dim, concat_axis=dim, tiled=True
+    )
 
 
 def expert_block(chosen, gate_matrix, up_matrix, down_matrix):
@@ -66,7 +74,7 @@
     outgoing = padded_rows[source_row].reshape(experts, capacity, width)
     arrived = lax.all_to_all(outgoing, "dev", split_axis=0, concat_axis=0, tiled=True)
     own_rows = arrived.reshape(experts * capacity, width)
-    both_rows = lax.all_gather(own_rows, "role", axis=0, tiled=True)
+    both_rows = gather_by_exchange(own_rows, "role", 0)
     expert_sum = lax.psum_scatter(
         expert_block(both_rows, w_gate[0], w_up[0], w_down[0]),
         "role",

time: 224 us -> 211 us (0.942)
  waiting for transfers between devices: 80.4 us -> 55.9 us
  blocking collectives: 57.5 us -> 69.3 us
  local copies, waits for them, and re-layouts: 14.2 us -> 17.6 us
  matrix products: 37.5 us -> 34.1 us
    all_gather x1 -> x0, waiting for transfers between devices: 19.5 us -> none  [per_device(): both_rows = lax.all_gather(own_rows, 'role', axis=0, tiled=True)]
    all_to_all x0 -> x1, blocking collectives: none -> 11.9 us  [gather_by_exchange(): lax.all_to_all(jnp.tile(value, repeats), axis, split_axis=dim, concat_axi...]
    reduce_scatter x1, waiting for transfers between devices: 28.2 us -> 23.2 us  [per_device(): lax.psum_scatter(expert_block(both_rows, w_gate[0], w_up[0], w_down[0]),...]
    dot_general x1, matrix products: 7.29 us -> 3.93 us  [expert_block(): up_part = jnp.dot(chosen, up_matrix, preferred_element_type=jnp.float32)]
    unnamed x12 -> x16, local copies, waits for them, and re-layouts: 0.94 us -> 3.89 us
  transfers between devices with their start and end apart: 3 -> 2, of which waited for: 3 -> 2; matrix products, arithmetic and copies ran while one was open for 7% -> 7% of each run, Pallas kernels for 0% -> 0%
where the time goes in v1:
time: 211 us
  blocking collectives  69.3 us (33%)
  waiting for transfers between devices  55.9 us (26%)
  matrix products  34.1 us (16%)
  local copies, waits for them, and re-layouts  17.6 us (8%)
  between operations  14.2 us (7%)
  starting transfers between devices  10.7 us (5%)
  other arithmetic  8.97 us (4%)
    all_to_all x1, blocking collectives, per_device(): lax.all_to_all(outgoing, 'dev', split_axis=0, concat_axis=0, tiled=True)  57.4 us
    all_to_all x1, waiting for transfers between devices, per_device(): lax.all_to_all(finished, 'dev', split_axis=0, concat_axis=0, tiled=True)  32.6 us
    reduce_scatter x1, waiting for transfers between devices, per_device(): lax.psum_scatter(expert_block(both_rows, w_gate[0], w_up[0], w_down[0]),...  23.2 us
    dot_general x1, matrix products, expert_block(): lax.dot_general(hidden_units, down_matrix, (((1,), (1,)), ((), ())), pref...  15.5 us
    all_to_all x1, blocking collectives, gather_by_exchange(): lax.all_to_all(jnp.tile(value, repeats), axis, split_axis=dim, concat_axi...  11.9 us
    all_to_all x1, starting transfers between devices, per_device(): lax.all_to_all(finished, 'dev', split_axis=0, concat_axis=0, tiled=True)  10.7 us
    dot_general x1, matrix products, attend_row(): jnp.dot(probs, cache_lat, preferred_element_type=jnp.float32)  6.34 us
    gather x1, local copies, waits for them, and re-layouts, per_device(): flat_back[destination].reshape(tok_count, topk_count, width)  6.04 us
  transfers between devices with their start and end apart: 2, of which 2 were waited for; matrix products, arithmetic and copies ran while one was open for 7% of the time, Pallas kernels for 0%

profile of v1, /device:TPU:1, one launch (start us, length us, event | category | flops | bytes accessed | tf_op | source)
XLA Modules:
  0.0 210.7 jit_solution(7105587924871440470)
XLA Ops:
  7.2 0.0 copy-start
  7.2 0.0 reduce-scatter.2.cloned.1.call-start
  7.2 0.8 copy.15
  8.1 0.1 eq.29
  8.2 0.1 eq.25
  8.2 0.7 broadcast_multiply_fusion
  9.0 0.6 reduce-window.6
  9.6 0.2 slice_reduce_fusion
  9.8 0.1 copy.14
  9.9 0.1 mul.42
  10.0 0.1 fusion.21
  10.1 1.4 scatter_custom_fusion
  11.5 1.0 concatenate.3
  12.5 4.2 %gather_fusion = bf16[512,3584]{1,0:T(8,128)(2,1)} fusion(bf16[33,3584]{1,0:T(8,128)(2,1)S(1)} %concatenate.3, s32[1024]{0:T(1024)S(1)} %pad_clamp_fusion.1), kind=kCustom, calls=%fused_computation | custom fusion | bytes 7342080 | tf_op jit(solution)/shard_map/gather | solution.py:74
  16.6 57.4 %all_to_all.19 = bf16[64,8,3584]{2,1,0:T(8,128)(2,1)S(1)} all-to-all(bf16[64,8,3584]{2,1,0:T(8,128)(2,1)} %bitcast.50), channel_id=1, replica_groups=mesh['role'=2,'dev'=64] {'dev'}, dimensions={0} | all-to-all | bytes 7340032 | tf_op jit(solution)/shard_map/all_to_all | solution.py:75
  74.1 0.5 tile.9
  74.5 0.0 copy-start.6
  74.5 11.9 %all_to_all.20 = bf16[2,512,3584]{2,1,0:T(8,128)(2,1)S(1)} all-to-all(bf16[2,512,3584]{2,1,0:T(8,128)(2,1)S(1)} %tile.9), channel_id=1, replica_groups=mesh['role'=2,'dev'=64] {'role'}, dimensions={0} | all-to-all | bytes 14680064 | tf_op jit(solution)/shard_map/all_to_all | solution.py:12
  86.4 0.0 copy-start.1
  86.5 2.9 %copy-done.1 = bf16[2,512,3584]{2,1,0:T(8,128)(2,1)} copy-done((bf16[2,512,3584]{2,1,0:T(8,128)(2,1)}, bf16[2,512,3584]{2,1,0:T(8,128)(2,1)S(1)}, u32[]{:S(2)}) %copy-start.1) | copy-done | bytes 7340056
  89.4 0.0 copy-done.6
  89.4 3.9 %fusion.4 = f32[1024,512]{1,0:T(8,128)S(1)} fusion(bf16[1024,3584]{1,0:T(8,128)(2,1)S(1)} %bitcast.52, bf16[1,3584,512]{2,1,0:T(8,128)(2,1)S(1)} %copy-done.6), kind=kOutput, calls=%fused_computation.8 | convolution fusion | flops 3758096384 | bytes 13107200 | tf_op jit(solution)/shard_map/dot_general | solution.py:19
  93.3 15.5 %fusion.2 = f32[1024,3584]{1,0:T(8,128)} fusion(bf16[1,3584,512]{2,1,0:T(8,128)(2,1)} %param.16, f32[1024,512]{1,0:T(8,128)S(1)} %fusion.4, bf16[1024,3584]{1,0:T(8,128)(2,1)} %bitcast.53, bf16[1,3584,512]{2,1,0:T(8,128)(2,1)} %param.14), kind=kOutput, calls=%fused_computation.6 | convolution fusion | flops 7519338496 | bytes 31457280 | tf_op jit(solution)/shard_map/dot_general | solution.py:21
  108.8 0.0 reduce-scatter.2.cloned.1.call-update
  108.8 23.2 %reduce-scatter.2.cloned.1.call-done = f32[512,3584]{1,0:T(8,128)} async-done(((f32[1024,3584]{1,0:T(8,128)}), f32[512,3584]{1,0:T(8,128)}) %reduce-scatter.2.cloned.1.call-update) | async-done | bytes 7340048 | tf_op jit(solution)/shard_map/reduce_scatter | solution.py:78
  132.1 5.3 %convert_bitcast_fusion = bf16[64,8,3584]{2,1,0:T(8,128)(2,1)} fusion(f32[512,3584]{1,0:T(8,128)} %reduce-scatter.2.cloned.1.call-done), kind=kLoop, calls=%fused_computation.12 | loop fusion | flops 1835008 | bytes 11010048 | tf_op jit(solution)/shard_map/reshape | solution.py:84
  137.3 0.0 copy-start.4
  137.3 0.0 copy-start.3
  137.3 0.0 copy-start.5
  137.3 0.0 copy-start.2
  137.3 10.7 %all-to-all-start.2 = ((bf16[64,8,3584]{2,1,0:T(8,128)(2,1)}), bf16[64,8,3584]{2,1,0:T(8,128)(2,1)}, u32[]{:S(2)}, u32[]{:S(2)}) async-start(bf16[64,8,3584]{2,1,0:T(8,128)(2,1)} %convert_bitcast_fusion), calls=%async_computation.3 | async-start | bytes 7340032 | tf_op jit(solution)/shard_map/all_to_all | solution.py:85
  148.0 0.0 copy-done.4
  148.0 0.1 copy.18
  148.1 0.0 copy-done.3
  148.1 0.1 reshape.96
  148.2 0.0 copy-done.5
  148.3 0.1 iota_compare_fusion.2
  148.3 0.0 copy-done.2
  148.4 6.0 %fusion.27 = f32[4,64,2048]{2,1,0:T(8,128)S(1)} fusion(bf16[4,64,512]{2,1,0:T(8,128)(2,1)S(1)} %copy-done.2, bf16[4,2048,512]{2,1,0:T(8,128)(2,1)} %param.19), kind=kOutput, calls=%fused_computation.47 | convolution fusion | flops 536870912 | bytes 10747904 | tf_op jit(solution)/shard_map/vmap()/dot_general | solution.py:29
  154.4 0.0 copy-done
  154.4 2.3 %fusion.26 = (f32[4,64]{1,0:T(4,128)S(1)}, f32[4,64,2048]{2,1,0:T(8,128)}) fusion(pred[4,2048]{1,0:T(4,128)(4,1)S(1)} %iota_compare_fusion.2, f32[4,64,2048]{2,1,0:T(8,128)S(1)} %fusion.27, bf16[4,64,64]{2,1,0:T(8,128)(2,1)S(1)} %reshape.96, bf16[4,64,2048]{2,1,0:T(8,128)(2,1)S(1)} %copy-done), kind=kOutput, calls=%fused_computation.46 | convolution fusion | flops 70256640 | bytes 5284864 | tf_op jit(solution)/shard_map/vmap()/sub | solution.py:40
  156.7 6.3 %convolution_convert_fusion = bf16[4,64,512]{2,1,0:T(8,128)(2,1)} fusion(bf16[4,2048,512]{2,1,0:T(8,128)(2,1)} %param.19, f32[4,64,2048]{2,1,0:T(8,128)} %get-tuple-element.3, f32[4,64]{1,0:T(4,128)S(1)} %get-tuple-element.2), kind=kOutput, calls=%fused_computation.21 | convolution fusion | flops 538050560 | bytes 10748928 | tf_op jit(solution)/shard_map/vmap()/dot_general | solution.py:42
  163.1 32.6 %all-to-all-done.2 = bf16[64,8,3584]{2,1,0:T(8,128)(2,1)} async-done(((bf16[64,8,3584]{2,1,0:T(8,128)(2,1)}), bf16[64,8,3584]{2,1,0:T(8,128)(2,1)}, u32[]{:S(2)}, u32[]{:S(2)}) %all-to-all-start.2) | async-done | bytes 3670048 | tf_op jit(solution)/shard_map/all_to_all | solution.py:85
  195.7 6.0 %gather_fusion.1 = bf16[256,3584]{1,0:T(8,128)(2,1)S(1)} fusion(bf16[512,3584]{1,0:T(8,128)(2,1)} %bitcast.10, s32[1024]{0:T(1024)S(1)} %pad_clamp_fusion), kind=kCustom, calls=%fused_computation.1 | custom fusion | bytes 3671040 | tf_op jit(solution)/shard_map/gather | solution.py:87
  201.7 2.1 %fusion.1 = bf16[32,3584]{1,0:T(8,128)(2,1)} fusion(bf16[256,3584]{1,0:T(8,128)(2,1)S(1)} %gather_fusion.1, f32[32,8]{1,0:T(8,128)S(1)} %copy.18), kind=kLoop, calls=%fused_computation.5 | loop fusion | flops 2637824 | bytes 2065408 | tf_op jit(solution)/shard_map/reduce_sum | solution.py:88
  (8 shorter events, 0.1 us)
Async XLA Ops:
  7.2 147.2 %copy-start = (bf16[4,64,2048]{2,1,0:T(8,128)(2,1)S(1)}, bf16[4,64,2048]{2,1,0:T(8,128)(2,1)}, u32[]{:S(2)}) copy-start(bf16[4,64,2048]{2,1,0:T(8,128)(2,1)} %param.20) | copy-start | bytes 3145732
  7.2 124.9 %reduce-scatter.2.cloned.1.call-start = ((), (), s32[]{:S(2)}) async-start(), calls=%async_computation.4 | async-start | bytes 22020096 | tf_op jit(solution)/shard_map/reduce_scatter | solution.py:78
  74.5 14.9 %copy-start.6 = (bf16[1,3584,512]{2,1,0:T(8,128)(2,1)S(1)}, bf16[1,3584,512]{2,1,0:T(8,128)(2,1)}, u32[]{:S(2)}) copy-start(bf16[1,3584,512]{2,1,0:T(8,128)(2,1)} %param.15) | copy-start | bytes 11010052
  86.4 2.9 %copy-start.1 = (bf16[2,512,3584]{2,1,0:T(8,128)(2,1)}, bf16[2,512,3584]{2,1,0:T(8,128)(2,1)S(1)}, u32[]{:S(2)}) copy-start(bf16[2,512,3584]{2,1,0:T(8,128)(2,1)S(1)} %all_to_all.20) | copy-start | bytes 22020100
  137.3 10.7 %copy-start.4 = (f32[32,8]{0,1:T(8,128)S(1)}, f32[32,8]{0,1:T(8,128)}, u32[]{:S(2)}) copy-start(f32[32,8]{0,1:T(8,128)} %param.13) | copy-start | bytes 3076
  137.3 10.8 %copy-start.3 = (bf16[4,4096]{1,0:T(4,128)(2,1)S(1)}, bf16[4,4096]{1,0:T(4,128)(2,1)}, u32[]{:S(2)}) copy-start(bf16[4,4096]{1,0:T(4,128)(2,1)} %param.18) | copy-start | bytes 98308
  137.3 10.9 %copy-start.5 = (s32[4]{0:T(128)S(1)}, s32[4]{0:T(128)}, u32[]{:S(2)}) copy-start(s32[4]{0:T(128)} %param.21) | copy-start | bytes 52
  137.3 11.0 %copy-start.2 = (bf16[4,64,512]{2,1,0:T(8,128)(2,1)S(1)}, bf16[4,64,512]{2,1,0:T(8,128)(2,1)}, u32[]{:S(2)}) copy-start(bf16[4,64,512]{2,1,0:T(8,128)(2,1)} %param.17) | copy-start | bytes 786436
  137.3 58.3 %all-to-all-start.2 = ((bf16[64,8,3584]{2,1,0:T(8,128)(2,1)}), bf16[64,8,3584]{2,1,0:T(8,128)(2,1)}, u32[]{:S(2)}, u32[]{:S(2)}) async-start(bf16[64,8,3584]{2,1,0:T(8,128)(2,1)} %convert_bitcast_fusion), calls=%async_computation.3 | async-start | bytes 7340032 | tf_op jit(solution)/shard_map/all_to_all | solution.py:85
Sparse Core Ops, SparseCore 0:
  108.9 23.0 reduce-scatter.1
